TPU v7x, 256 devices: a whole 4x4x8 slice. The times are simulated.
256 devices in a mesh: outer: 4 (over y_lo, core), inner: 64 (over x, y_hi, z).
Axes of the slice: x: 4, y: 4 (y_hi: 2, y_lo: 2; y = y_hi * 2 + y_lo), z: 8, core: 2. Of those that a mesh axis runs over, the one named last changes fastest.
Arguments:
- layer_input: bfloat16 [8192, 256, 192], P(('outer', 'inner')), may hold values from -6 to 6
- out_grad: bfloat16 [8192, 256, 192], P(('outer', 'inner')), may hold values from -6 to 6
- mix_weight: bfloat16 [256, 128], replicated, may hold values from -0.375 to 0.375
- lift_weight: bfloat16 [128, 192], replicated, may hold values from -0.5 to 0.5
- linear_weight: bfloat16 [256, 256], replicated, may hold values from -0.375 to 0.375
- row_ids: int32 [8192, 256], P(('outer', 'inner')), may hold values from 0 to 131071, as said below
- row_home: int32 [131072], replicated, may hold values from 0 to 131071, as said below
- table: float32 [131072, 192], P('inner'), may hold values from -0.6 to 0.6
- row_accum: float32 [131072], P('inner'), may hold values from 1 to 100
Outputs:
- new_table: float32 [131072, 192], P('inner')
- new_accum: float32 [131072], P('inner')
- mix_grad: float32 [256, 128], replicated
- lift_grad: float32 [128, 192], replicated
- linear_grad: float32 [256, 256], replicated
Inputs may be any that keep to these rules, and one draw needn't show every extreme that they name: row_home is a permutation: hashed row i is stored at position row_home[i], held by inner index row_home[i] // 2048. In each aligned block of 16 samples (all their features together), every inner index is the owner, row_home[row_ids] // 2048, of exactly 64 lookups. The same row may be named many times.
All inputs are finite; a program needn't handle non-finite values.
Results may differ from a plain program's by a relative error of at most 0.0041.
Values may be sent and summed in bfloat16 or wider, within the bound.
A program may use at most 64 MiB of HBM per device.

v0:
```python
import math

import jax
import jax.numpy as jnp
from jax import lax
from jax.sharding import PartitionSpec as P

LEARN_RATE = 0.5


def interaction_grads(inputs, cotangent, mix_weight, lift_weight, linear_weight, scaling):
    compressed = jnp.einsum(
        "bfd,fk->bdk", inputs, mix_weight, preferred_element_type=jnp.float32
    ).astype(jnp.bfloat16)
    products = (
        jnp.einsum("bfd,bdk->bfk", inputs, compressed, preferred_element_type=jnp.float32) * scaling
    ).astype(jnp.bfloat16)
    d_products = jnp.einsum(
        "bfd,kd->bfk", cotangent, lift_weight, preferred_element_type=jnp.float32
    ).astype(jnp.bfloat16)
    d_compressed = (
        jnp.einsum("bfd,bfk->bdk", inputs, d_products, preferred_element_type=jnp.float32) * scaling
    ).astype(jnp.bfloat16)
    d_inputs = cotangent.astype(jnp.float32)
    d_inputs = d_inputs + jnp.einsum(
        "fg,bfd->bgd", linear_weight, cotangent, preferred_element_type=jnp.float32
    )
    d_inputs = d_inputs + scaling * jnp.einsum(
        "bfk,bdk->bfd", d_products, compressed, preferred_element_type=jnp.float32
    )
    d_inputs = d_inputs + jnp.einsum(
        "fk,bdk->bfd", mix_weight, d_compressed, preferred_element_type=jnp.float32
    )
    g_mix = jnp.einsum("bfd,bdk->fk", inputs, d_compressed, preferred_element_type=jnp.float32)
    g_lift = jnp.einsum("bfk,bfd->kd", products, cotangent, preferred_element_type=jnp.float32)
    g_linear = jnp.einsum("bfd,bgd->fg", cotangent, inputs, preferred_element_type=jnp.float32)
    rows_out = d_inputs.astype(jnp.bfloat16).reshape(-1, d_inputs.shape[2])
    return (rows_out, (g_mix, g_lift, g_linear))


def adagrad(weights, history, gradient):
    updated = history + jnp.mean(gradient * gradient, axis=1)
    return (weights - LEARN_RATE * gradient / jnp.sqrt(updated)[:, None], updated)


def owner_ranks(owner_of, owners):
    lookups = owner_of.shape[0]
    width = math.gcd(lookups, 128)
    groups = lookups // width
    hot = (owner_of[:, None] == jnp.arange(owners, dtype=jnp.int32)[None, :]).astype(jnp.bfloat16)
    hot = hot.reshape(groups, width, owners)
    lower = (jnp.arange(width)[:, None] > jnp.arange(width)[None, :]).astype(jnp.bfloat16)
    within = jnp.einsum("ij,gjo->gio", lower, hot, preferred_element_type=jnp.float32)
    totals = jnp.sum(hot.astype(jnp.float32), axis=1)
    before = jnp.cumsum(totals, axis=0) - totals
    counted = jnp.sum(hot.astype(jnp.float32) * (within + before[:, None, :]), axis=2)
    return counted.reshape(-1).astype(jnp.int32)


def add_rows(collected, slots, values):
    count = values.shape[0]
    table_rows = collected.shape[0]
    width = math.gcd(count, 2048)
    columns = jnp.arange(table_rows, dtype=jnp.int32)
    for block_index in range(count // width):
        start = block_index * width
        hot = (slots[start : start + width, None] == columns[None, :]).astype(jnp.bfloat16)
        collected = collected + jnp.einsum(
            "lr,ld->rd", hot, values[start : start + width], preferred_element_type=jnp.float32
        )
    return collected


def on_device(
    layer_input,
    out_grad,
    mix_weight,
    lift_weight,
    linear_weight,
    row_ids,
    row_home,
    table,
    row_accum,
):
    owners = lax.axis_size("inner")
    sample_count, feature_count, embed_width = layer_input.shape
    table_rows = table.shape[0]
    lookups = sample_count * feature_count
    per_owner = lookups // (2 * owners)
    scaling = 1.0 / math.sqrt(embed_width)
    placed = jnp.take(row_home, row_ids.reshape(-1), axis=0)
    owner_of = placed // table_rows
    target = owner_of * (2 * per_owner) + owner_ranks(owner_of, owners)
    ordering = jnp.zeros((lookups,), jnp.int32).at[target].set(jnp.arange(lookups, dtype=jnp.int32))
    ordering = ordering.reshape(owners, 2, per_owner)
    local_rows = (
        jnp.zeros((lookups,), jnp.int32)
        .at[target]
        .set(placed % table_rows)
        .reshape(owners, 2 * per_owner)
    )
    arrived_rows = lax.all_to_all(
        local_rows, "inner", split_axis=0, concat_axis=0, tiled=True
    ).reshape(owners, 2, per_owner)
    collected = jnp.zeros((table_rows, embed_width), jnp.float32)
    rows_out, totals = interaction_grads(
        layer_input, out_grad, mix_weight, lift_weight, linear_weight, scaling
    )
    outgoing = jnp.take(rows_out, ordering.reshape(-1), axis=0).reshape(
        owners, 2 * per_owner, embed_width
    )
    incoming = lax.all_to_all(outgoing, "inner", split_axis=0, concat_axis=0, tiled=True)
    collected = add_rows(collected, arrived_rows.reshape(-1), incoming.reshape(-1, embed_width))
    batch_total = sample_count * lax.axis_size("outer") * owners
    summed = lax.psum((totals[0], totals[1], totals[2]), ("outer", "inner"))
    mix_grad = summed[0] / batch_total
    lift_grad = summed[1] / batch_total
    linear_grad = summed[2] / batch_total
    complete = lax.psum(collected, "outer")
    new_table, new_accum = adagrad(table, row_accum, complete)
    return (new_table, new_accum, mix_grad, lift_grad, linear_grad)


def solution(mesh):
    placed = (
        P(("outer", "inner"), None, None),
        P(("outer", "inner"), None, None),
        P(),
        P(),
        P(),
        P(("outer", "inner"), None),
        P(),
        P("inner", None),
        P("inner"),
    )
    return jax.shard_map(
        on_device,
        mesh=mesh,
        in_specs=placed,
        out_specs=(P("inner", None), P("inner"), P(), P(), P()),
        check_vma=False,
    )
```

profile of v0, /device:TPU:15, one launch (start us, length us, event | category | flops | bytes accessed | tf_op | source)
XLA Modules:
  0.0 606.4 jit_solution(2677957759859553030)
XLA Ops:
  7.2 0.0 copy-start
  7.2 0.9 reshape.231
  8.1 0.8 copy.40
  8.9 0.8 copy.39
  9.8 103.6 %gather_fusion = s32[8192]{0:T(1024)S(1)} fusion(s32[131072]{0:T(1024)} %param.15, s32[8192]{0:T(1024)S(1)} %broadcast_clamp_fusion), kind=kCustom, calls=%fused_computation | custom fusion | bytes 98304 | tf_op jit(solution)/shard_map/jit(_take)/gather | solution.py:91
  113.4 0.0 copy-start.5
  113.5 0.6 convert_reduce_fusion
  114.1 0.1 reduce_window_sum.11
  114.2 0.9 fusion.13
  115.1 0.3 compare_select_fusion
  115.4 31.0 %scatter_custom_fusion = s32[8192]{0:T(1024)} fusion(s32[8192]{0:T(1024)S(1)} %bitcast.114, s32[8192]{0:T(1024)S(1)} %add_select_fusion, s32[]{:T(128)} %constant.65.clone.1), kind=kCustom, calls=%fused_computation.94 | custom fusion | bytes 32772 | tf_op jit(solution)/shard_map/scatter | solution.py:99
  146.4 13.3 %all-to-all-start = ((s32[64,1,128]{2,1,0:T(1,128)}), s32[64,1,128]{2,1,0:T(1,128)S(1)}, u32[]{:S(2)}, u32[]{:S(2)}) async-start(s32[64,1,128]{2,1,0:T(1,128)} %bitcast.7), calls=%async_computation | async-start | bytes 65536 | tf_op jit(solution)/shard_map/all_to_all | solution.py:102
  159.8 30.7 %scatter_custom_fusion.1 = s32[8192]{0:T(1024)S(1)} fusion(s32[8192]{0:T(1024)S(1)} %bitcast.115, s32[8192]{0:T(1024)S(1)} %iota.26, s32[]{:T(128)} %constant.65.clone.1), kind=kCustom, calls=%fused_computation.92 | custom fusion | bytes 32772 | tf_op jit(solution)/shard_map/scatter | solution.py:94
  190.5 1.0 convolution_convert_fusion.1
  191.5 0.8 copy-done.1
  192.3 1.3 convolution_convert_fusion
  193.7 1.0 multiply_convert_fusion.1
  194.7 1.0 fusion.54
  195.7 0.1 copy-done.6
  195.7 1.0 fusion.36
  196.7 3.1 fusion.8
  199.8 6.1 %copy.33 = bf16[32,256,192]{2,1,0:T(8,128)(2,1)} copy(bf16[32,256,192]{1,2,0:T(8,128)(2,1)} %fusion.8) | data formatting | bytes 6291456 | tf_op jit(solution)/shard_map/reshape | solution.py:37
  205.9 33.8 %gather_fusion.1 = bf16[8192,192]{1,0:T(8,128)(2,1)} fusion(bf16[8192,192]{1,0:T(8,128)(2,1)} %bitcast.104, s32[8192]{0:T(1024)S(1)} %fusion.46), kind=kCustom, calls=%fused_computation.1 | custom fusion | bytes 6324224 | tf_op jit(solution)/shard_map/jit(_take)/gather | solution.py:109
  239.7 6.0 copy.25
  245.7 3.9 broadcast_select_fusion
  249.6 12.4 %all-to-all-start.1 = ((bf16[64,128,192]{1,2,0:T(8,128)(2,1)}), bf16[64,128,192]{1,2,0:T(8,128)(2,1)}, u32[]{:S(2)}, u32[]{:S(2)}) async-start(bf16[64,128,192]{1,2,0:T(8,128)(2,1)} %broadcast_select_fusion), calls=%async_computation.1 | async-start | bytes 6291456 | tf_op jit(solution)/shard_map/all_to_all | solution.py:112
  261.9 0.0 all-reduce.6.cloned.1.call-start
  262.0 2.9 fusion.21
  264.9 1.7 convolution_bitcast_fusion
  266.7 4.7 fusion.24
  271.3 0.0 all-reduce.6.cloned.1.call-update
  271.4 0.3 all-reduce.4.cloned.1.call-start
  271.6 60.4 %all-to-all-done.1 = bf16[64,128,192]{1,2,0:T(8,128)(2,1)} async-done(((bf16[64,128,192]{1,2,0:T(8,128)(2,1)}), bf16[64,128,192]{1,2,0:T(8,128)(2,1)}, u32[]{:S(2)}, u32[]{:S(2)}) %all-to-all-start.1) | async-done | bytes 3145760 | tf_op jit(solution)/shard_map/all_to_all | solution.py:112
  332.0 2.1 slice_bitcast_fusion
  334.1 3.5 fusion
  337.6 3.5 fusion.12
  341.2 3.5 fusion.11
  344.7 4.7 fusion.10
  349.4 0.0 all-reduce.4.cloned.1.call-update
  349.4 188.0 %all-reduce.6.cloned.1.call-done = (f32[256,128]{0,1:T(8,128)}, f32[128,192]{0,1:T(8,128)}, f32[256,256]{1,0:T(8,128)}) async-done(((f32[256,128]{0,1:T(8,128)}, f32[128,192]{0,1:T(8,128)}, f32[256,256]{1,0:T(8,128)}), (f32[256,128]{0,1:T(8,128)}, f32[128,192]{0,1:T(8,128)}, f32[256,256]{1,0:T(8,128)})) %all-reduce.6.cloned.1.call-update) | async-done | bytes 491536 | tf_op jit(solution)/shard_map/psum | solution.py:115
  537.4 0.9 broadcast_multiply_fusion.1
  538.3 0.8 copy.31
  539.1 1.5 broadcast_multiply_fusion.2
  540.6 1.7 broadcast_multiply_fusion
  542.3 51.8 %all-reduce.4.cloned.1.call-done = f32[2048,192]{0,1:T(8,128)} async-done(((f32[2048,192]{0,1:T(8,128)}), f32[2048,192]{0,1:T(8,128)}) %all-reduce.4.cloned.1.call-update) | async-done | bytes 1572880 | tf_op jit(solution)/shard_map/psum | solution.py:119
  594.1 1.5 multiply_reduce_fusion
  595.6 0.6 fusion.52
  596.2 3.3 divide_subtract_fusion
  (25 shorter events, 0.2 us)
Async XLA Ops:
  7.2 183.3 %copy-start = (bf16[32,256,192]{1,2,0:T(8,128)(2,1)S(1)}, bf16[32,256,192]{1,2,0:T(8,128)(2,1)}, u32[]{:S(2)}) copy-start(bf16[32,256,192]{1,2,0:T(8,128)(2,1)} %param.9) | copy-start | bytes 9437188
  113.4 77.1 %copy-start.5 = (bf16[256,128]{1,0:T(8,128)(2,1)S(1)}, bf16[256,128]{1,0:T(8,128)(2,1)}, u32[]{:S(2)}) copy-start(bf16[256,128]{1,0:T(8,128)(2,1)} %param.11) | copy-start | bytes 196612
  115.1 76.4 %copy-start.7 = (bf16[128,192]{0,1:T(8,128)(2,1)S(1)}, bf16[128,192]{0,1:T(8,128)(2,1)}, u32[]{:S(2)}) copy-start(bf16[128,192]{0,1:T(8,128)(2,1)} %param.12) | copy-start | bytes 147460
  146.4 103.2 %all-to-all-start = ((s32[64,1,128]{2,1,0:T(1,128)}), s32[64,1,128]{2,1,0:T(1,128)S(1)}, u32[]{:S(2)}, u32[]{:S(2)}) async-start(s32[64,1,128]{2,1,0:T(1,128)} %bitcast.7), calls=%async_computation | async-start | bytes 65536 | tf_op jit(solution)/shard_map/all_to_all | solution.py:102
  190.4 1.9 copy-start.1
  192.3 2.3 copy-start.4
  194.7 2.0 copy-start.3
  194.7 1.0 copy-start.6
  249.6 82.5 %all-to-all-start.1 = ((bf16[64,128,192]{1,2,0:T(8,128)(2,1)}), bf16[64,128,192]{1,2,0:T(8,128)(2,1)}, u32[]{:S(2)}, u32[]{:S(2)}) async-start(bf16[64,128,192]{1,2,0:T(8,128)(2,1)} %broadcast_select_fusion), calls=%async_computation.1 | async-start | bytes 6291456 | tf_op jit(solution)/shard_map/all_to_all | solution.py:112
  261.9 275.4 %all-reduce.6.cloned.1.call-start = ((), (), s32[]{:S(2)}) async-start(), calls=%async_computation.3 | async-start | bytes 983040 | tf_op jit(solution)/shard_map/psum | solution.py:115
  262.0 2.9 copy-start.2
  271.4 322.7 %all-reduce.4.cloned.1.call-start = ((), (), s32[]{:S(2)}) async-start(), calls=%async_computation.2 | async-start | bytes 3145728 | tf_op jit(solution)/shard_map/psum | solution.py:119
  349.4 246.2 %copy-start.8 = (f32[2048]{0:T(1024)S(1)}, f32[2048]{0:T(1024)}, u32[]{:S(2)}) copy-start(f32[2048]{0:T(1024)} %param.17) | copy-start | bytes 24580
Sparse Core Ops, SparseCore 0:
  271.5 265.8 all-reduce.5
  540.6 53.3 all-reduce.3
where the time goes:
time: 613 us; the launch traced here: 606 us
  waiting for transfers between devices  300 us (49%)
  local copies, waits for them, and re-layouts  218 us (36%)
  matrix products  33.7 us (5%)
  starting transfers between devices  26 us (4%)
  other arithmetic  14.6 us (2%)
  between operations  14.3 us (2%)
    psum x1, waiting for transfers between devices, on_device(): summed = lax.psum((totals[0], totals[1], totals[2]), ('outer', 'inner'))  188 us
    gather x1, local copies, waits for them, and re-layouts, on_device(): placed = jnp.take(row_home, row_ids.reshape(-1), axis=0)  104 us
    all_to_all x1, waiting for transfers between devices, on_device(): lax.all_to_all(outgoing, 'inner', split_axis=0, concat_axis=0, tiled=True)  60.4 us
    psum x1, waiting for transfers between devices, on_device(): complete = lax.psum(collected, 'outer')  51.8 us
    gather x2, local copies, waits for them, and re-layouts, on_device(): jnp.take(rows_out, ordering.reshape(-1), axis=0)  39.8 us
    scatter x1, local copies, waits for them, and re-layouts, on_device(): local_rows = jnp.zeros((lookups,), jnp.int32).at[target].set(placed % tab...  31 us
    scatter x1, local copies, waits for them, and re-layouts, on_device(): jnp.zeros((lookups,), jnp.int32).at[target]  30.7 us
    dot_general x4, matrix products, add_rows(): jnp.einsum('lr,ld->rd', hot, values[start:start + width], preferred_eleme...  15.2 us
  transfers between devices with their start and end apart: 4, of which 3 were waited for; matrix products, arithmetic and copies ran while one was open for 20% of the time, Pallas kernels for 0%

commit v1 on v0

v1 whole, which is shorter than its diff:
```python
import math

import jax
import jax.numpy as jnp
from jax import lax
from jax.experimental import pallas as pl
from jax.experimental.pallas import tpu as pltpu
from jax.sharding import PartitionSpec as P

LEARN_RATE = 0.5
MESH = pl.DeviceIdType.MESH
BF = jnp.bfloat16
F32 = jnp.float32
VM = pl.BlockSpec(memory_space=pltpu.VMEM)

SAMPLES, FEATS, WIDTH, RANK = 32, 256, 192, 128
BATCH = 8192
HALF = 4096
PACK = 1536
PIECE = 768


def dot(a, b, dims=((1,), (0,))):
    return lax.dot_general(a, b, (dims, ((), ())), preferred_element_type=F32)


NT = ((1,), (1,))


def iota(shape, axis):
    return lax.broadcasted_iota(jnp.int32, shape, axis)


def index_kernel(ids_ref, home_ref, key_ref, local_ref, table_t, place_ref):
    home = home_ref[...]
    high = (home >> 9).astype(F32)
    low = ((home & 511) - 256).astype(F32)
    table_t[0:128, :] = high.T.astype(BF)
    table_t[128:256, :] = low.T.astype(BF)
    rows1024 = iota((1024, 256), 0)
    rows128 = iota((128, 256), 0)

    def look(b, carry):
        ids = ids_ref[pl.ds(b, 1), :]
        hot = (rows1024 == (ids >> 7)).astype(F32).astype(BF)
        found = dot(table_t[...], hot)
        mask = rows128 == (ids & 127)
        high_part = jnp.sum(jnp.where(mask, found[0:128], 0.0), axis=0, keepdims=True)
        low_part = jnp.sum(jnp.where(mask, found[128:256], 0.0), axis=0, keepdims=True)
        place_ref[pl.ds(b, 1), :] = (high_part * 512.0 + low_part + 256.0).astype(jnp.int32)
        return carry

    lax.fori_loop(0, SAMPLES, look, 0, unroll=4)
    upper = (iota((256, 256), 0) < iota((256, 256), 1)).astype(F32).astype(BF)
    rows64 = iota((64, 256), 0)
    for half in range(2):

        def rank(step, carry):
            counts, firsts = carry
            b = half * 16 + step
            place = place_ref[pl.ds(b, 1), :]
            owner = place >> 11
            local = place & 2047
            own = (rows64 == owner).astype(F32)
            before = dot(own.astype(BF), upper) + counts
            rank_of = jnp.sum(own * before, axis=0, keepdims=True).astype(jnp.int32)
            key_ref[pl.ds(b, 1), :] = (owner & 7) * 512 + (owner >> 3) * 64 + rank_of
            hot = (rows64 == rank_of).astype(F32).astype(BF)
            parts = jnp.concatenate(
                [own * (local >> 4).astype(F32), own * (local & 15).astype(F32)], axis=0
            ).astype(BF)
            firsts = firsts + dot(parts, hot, NT)
            counts = counts + jnp.sum(own, axis=1, keepdims=True)
            return counts, firsts

        start = (jnp.zeros((64, 1), F32), jnp.zeros((128, 64), F32))
        unused, firsts = lax.fori_loop(0, 16, rank, start, unroll=4)
        merged = firsts[0:64] * 16.0 + firsts[64:128]
        local_ref[:, half * 64 : (half + 1) * 64] = merged.astype(jnp.int32)


def index_call(row_ids, home):
    return pl.pallas_call(
        index_kernel,
        out_shape=(
            jax.ShapeDtypeStruct((SAMPLES, FEATS), jnp.int32),
            jax.ShapeDtypeStruct((64, 128), jnp.int32),
        ),
        in_specs=[VM, VM],
        out_specs=(VM, VM),
        scratch_shapes=[pltpu.VMEM((256, 1024), BF), pltpu.VMEM((SAMPLES, FEATS), jnp.int32)],
        compiler_params=pltpu.CompilerParams(vmem_limit_bytes=32 * 2**20),
        name="index",
    )(row_ids, home)


def layer_kernel(x_ref, g_ref, mix_ref, mix_t_ref, lift_ref, lift_t_ref, linear_t_ref, rows_ref, dense_ref):
    scaling = 1.0 / math.sqrt(WIDTH)

    @pl.when(pl.program_id(0) == 0)
    def _():
        dense_ref[...] = jnp.zeros_like(dense_ref)

    x = x_ref[0]
    g = g_ref[0]
    d_products = dot(g, lift_t_ref[...]).astype(BF)
    d_products_t = dot(lift_ref[...], g, NT).astype(BF)
    both = dot(jnp.concatenate([mix_t_ref[...], d_products_t], axis=0), x)
    compressed_t = both[0:128].astype(BF)
    d_compressed_t = (both[128:256] * scaling).astype(BF)
    products_t = (dot(compressed_t, x, NT) * scaling).astype(BF)
    d_inputs = g.astype(F32) + dot(linear_t_ref[...], g)
    d_inputs = d_inputs + scaling * dot(d_products, compressed_t)
    d_inputs = d_inputs + dot(mix_ref[...], d_compressed_t)
    rows_ref[...] = jnp.concatenate([d_inputs, d_inputs[:, 128:192]], axis=1).astype(BF)
    dense_ref[0:256] += dot(x, d_compressed_t, NT)
    linear = dot(g, x, NT)
    dense_ref[256:512] += linear[:, 0:128]
    dense_ref[512:768] += linear[:, 128:256]
    lift = dot(products_t, g)
    dense_ref[768:896] += lift[:, 0:128]
    dense_ref[896:1024, 0:64] += lift[:, 128:192]


def layer_call(x, g, mix, lift, linear):
    whole = lambda shape: pl.BlockSpec(shape, lambda b: (0, 0))
    return pl.pallas_call(
        layer_kernel,
        grid=(SAMPLES,),
        out_shape=(
            jax.ShapeDtypeStruct((SAMPLES * FEATS, 256), BF),
            jax.ShapeDtypeStruct((1024, 128), F32),
        ),
        in_specs=[
            pl.BlockSpec((1, FEATS, WIDTH), lambda b: (b, 0, 0)),
            pl.BlockSpec((1, FEATS, WIDTH), lambda b: (b, 0, 0)),
            whole((256, 128)),
            whole((128, 256)),
            whole((128, 192)),
            whole((192, 128)),
            whole((256, 256)),
        ],
        out_specs=(pl.BlockSpec((FEATS, 256), lambda b: (b, 0)), whole((1024, 128))),
        compiler_params=pltpu.CompilerParams(
            vmem_limit_bytes=32 * 2**20, dimension_semantics=("arbitrary",)
        ),
        name="layer",
    )(x, g, mix, mix.T, lift, lift.T, linear.T)


class Spot:
    def __init__(self):
        outer = lax.axis_index("outer")
        inner = lax.axis_index("inner")
        self.core = lax.rem(outer, 2)
        self.y_lo = outer // 2
        self.x = inner // 16
        self.y_hi = lax.rem(inner // 8, 2)
        self.z = lax.rem(inner, 8)
        self.y = self.y_hi * 2 + self.y_lo

    def at(self, x=None, y=None, z=None, core=None):
        x = self.x if x is None else x
        y = self.y if y is None else y
        z = self.z if z is None else z
        core = self.core if core is None else core
        return (lax.rem(y, 2) * 2 + core, (x * 2 + y // 2) * 8 + z)


def chunk_offset(i):
    return 4 + (1 - 2 * (i % 2)) * ((i + 1) // 2)


def exchange_kernel(
    key_ref, local_ref, rows_ref, dense_ref, table_ref, accum_ref,
    new_table_ref, new_accum_ref, mix_ref, lift_ref, linear_ref,
    send, recv, local_in, rhs, own, across, across_in, ring_out, ring_in,
    finish, chip_in, core_in, core_in2,
    d_half, d_half_in, d_y_in, d_y, d_x_in, d_z, d_xg, d_yg, d_cg,
    s_send, s_recv, i_send, i_recv, a_send, a_recv, r_send, r_recv, f_send, f_recv, d_send, d_recv,
):
    me = Spot()
    x, y, z, core = me.x, me.y, me.z, me.core
    lanes = iota((256, 128), 1)
    iota_rows = iota((256, 128), 0).astype(F32).astype(BF)

    def peer(k):
        dx, dy = k // 2, k % 2
        y_to = me.y if dy == 0 else (1 - me.y_hi) * 2 + (1 - me.y_lo)
        return me.at(x=lax.rem(x + dx, 4), y=y_to)

    def place_of(k):
        dx, dy = k // 2, k % 2
        return lax.rem(x + dx, 4) * 2 + (me.y_hi if dy == 0 else 1 - me.y_hi)

    partner = me.at(core=1 - core)
    beside = me.at(y=me.y_hi * 2 + 1 - me.y_lo)
    up = me.at(z=lax.rem(z + 1, 8))
    down = me.at(z=lax.rem(z + 7, 8))
    y_peer = lambda k: me.at(y=lax.rem(y + k, 4))
    x_peer = lambda k: me.at(x=lax.rem(x + k, 4))
    z_peer = lambda k: me.at(z=lax.rem(z + k, 8))

    barrier = pltpu.get_barrier_semaphore()
    greeted = (
        [peer(k) for k in range(1, 8)]
        + [partner]
        + [y_peer(k) for k in (1, 2, 3)]
        + [x_peer(k) for k in (1, 2, 3)]
        + [z_peer(k) for k in range(1, 8)]
    )
    for device in greeted:
        pl.semaphore_signal(barrier, inc=1, device_id=device, device_id_type=MESH)
    pl.semaphore_wait(barrier, len(greeted))

    def copy(src, dst, send_sem, recv_sem, device):
        return pltpu.make_async_remote_copy(
            src_ref=src, dst_ref=dst, send_sem=send_sem, recv_sem=recv_sem,
            device_id=device, device_id_type=MESH,
        )

    def index_copy(k):
        return copy(local_ref.at[place_of(k)], local_in.at[k], i_send.at[k], i_recv.at[k], peer(k))

    def lookup_copy(i, k):
        return copy(send.at[i, place_of(k)], recv.at[i, k], s_send.at[i, k], s_recv.at[i, k], peer(k))

    def across_copy(i):
        return copy(across.at[i], across_in.at[i], a_send.at[i], a_recv.at[i], partner)

    def ring_copy(way, slot):
        return copy(
            ring_out.at[way, slot], ring_in.at[way, slot], r_send.at[way, slot], r_recv.at[way, slot],
            (up, down)[way],
        )

    def chip_copy(p):
        return copy(finish.at[p], chip_in.at[p], f_send.at[0, p], f_recv.at[0, p], beside)

    def core_copy(p):
        return copy(finish.at[p], core_in.at[p], f_send.at[1, p], f_recv.at[1, p], partner)

    def forward_copy(p):
        return copy(chip_in.at[p], core_in2.at[p], f_send.at[2, p], f_recv.at[2, p], partner)

    def half_copy():
        return copy(dense_ref.at[1 - core], d_half_in, d_send.at[0], d_recv.at[0], partner)

    def y_copy(k):
        return copy(d_half.at[lax.rem(y + k, 4)], d_y_in.at[k - 1], d_send.at[k], d_recv.at[k], y_peer(k))

    def x_copy(k):
        return copy(d_y.at[lax.rem(x + k, 4)], d_x_in.at[k - 1], d_send.at[3 + k], d_recv.at[3 + k], x_peer(k))

    def z_copy(k):
        return copy(d_z.at[z], d_z.at[z], d_send.at[6 + k], d_recv.at[6 + k], z_peer(k))

    def z_wait(k):
        return copy(d_z.at[z], d_z.at[lax.rem(z + 8 - k, 8)], d_send.at[6 + k], d_recv.at[6 + k], z_peer(k))

    def xg_copy(k):
        return copy(d_xg.at[x], d_xg.at[x], d_send.at[13 + k], d_recv.at[13 + k], x_peer(k))

    def xg_wait(k):
        return copy(d_xg.at[x], d_xg.at[lax.rem(x + 4 - k, 4)], d_send.at[13 + k], d_recv.at[13 + k], x_peer(k))

    def yg_copy(k):
        return copy(d_yg.at[y], d_yg.at[y], d_send.at[16 + k], d_recv.at[16 + k], y_peer(k))

    def yg_wait(k):
        return copy(d_yg.at[y], d_yg.at[lax.rem(y + 4 - k, 4)], d_send.at[16 + k], d_recv.at[16 + k], y_peer(k))

    def cg_copy():
        return copy(d_cg.at[core], d_cg.at[core], d_send.at[20], d_recv.at[20], partner)

    def cg_wait():
        return copy(d_cg.at[core], d_cg.at[1 - core], d_send.at[20], d_recv.at[20], partner)

    def dense_1():
        half_copy().start()

    def dense_2():
        half_copy().wait_recv()
        total = dense_ref[core] + d_half_in[...]
        d_half[...] = total.reshape(4, 128, 128)
        for k in (1, 2, 3):
            y_copy(k).start()

    def dense_3():
        for k in (1, 2, 3):
            y_copy(k).wait_recv()
        total = d_half[y] + d_y_in[0] + d_y_in[1] + d_y_in[2]
        d_y[...] = total.reshape(4, 32, 128)
        for k in (1, 2, 3):
            x_copy(k).start()

    def dense_4():
        for k in (1, 2, 3):
            x_copy(k).wait_recv()
        d_z[z] = d_y[x] + d_x_in[0] + d_x_in[1] + d_x_in[2]
        for k in range(1, 8):
            z_copy(k).start()

    def dense_5():
        for k in range(1, 8):
            z_wait(k).wait_recv()
        total = d_z[0]
        for k in range(1, 8):
            total = total + d_z[k]
        d_xg[x] = total * (1.0 / BATCH)
        for k in (1, 2, 3):
            xg_copy(k).start()

    def dense_6():
        for k in (1, 2, 3):
            xg_wait(k).wait_recv()
        d_yg[y] = d_xg[...].reshape(128, 128)
        for k in (1, 2, 3):
            yg_copy(k).start()

    def dense_7():
        for k in (1, 2, 3):
            yg_wait(k).wait_recv()
        d_cg[core] = d_yg[...].reshape(512, 128)
        cg_copy().start()

    def dense_8():
        cg_wait().wait_recv()
        mix_ref[...] = d_cg[0, 0:256]
        linear_ref[:, 0:128] = d_cg[0, 256:512]
        linear_ref[:, 128:256] = d_cg[1, 0:256]
        lift_ref[:, 0:128] = d_cg[1, 256:384]
        lift_ref[:, 128:192] = d_cg[1, 384:512, 0:64]

    def one_hot(row, base):
        near = (row - base).astype(F32).astype(BF)
        tiles = []
        for t in range(row.shape[1] // 128):
            part = jnp.broadcast_to(near[:, t * 128 : (t + 1) * 128], (256, 128))
            tiles.append(jnp.where(iota_rows == part, jnp.ones((), BF), jnp.zeros((), BF)))
        return jnp.concatenate(tiles, axis=1)

    def sort_chunk(i):
        to = lax.rem(z + chunk_offset(i), 8)
        for part in range(2):
            base = to * 512 + part * 256
            got = []
            for half in range(2):
                total = jnp.zeros((256, 256), F32)
                for t in range(4):
                    hot = jnp.concatenate(
                        [
                            one_hot(key_ref[pl.ds(half * 16 + t * 4 + b, 1), :], base)
                            for b in range(4)
                        ],
                        axis=1,
                    )
                    start = half * HALF + t * 1024
                    total = total + dot(hot, rows_ref[start : start + 1024, :])
                got.append(total)
            tail = jnp.where(lanes < 64, got[0][:, 128:256], got[1][:, 128:256]).astype(BF)
            for q in range(4):
                at = slice(q * 64, (q + 1) * 64)
                send[i, part * 4 + q, 0:64, :] = got[0][at, 0:128].astype(BF)
                send[i, part * 4 + q, 64:128, :] = got[1][at, 0:128].astype(BF)
                send[i, part * 4 + q, 128:192, :] = tail[at]

    def add_chunk(i):
        to = lax.rem(z + chunk_offset(i), 8)
        lane64 = iota((64, 128), 1) < 64
        where = []
        for k in range(8):
            if k == 0:
                block = send.at[i, place_of(0)]
                where.append(local_ref[place_of(0), pl.ds(to, 1), :])
            else:
                lookup_copy(i, k).wait_recv()
                block = recv.at[i, k]
                where.append(local_in[k, pl.ds(to, 1), :])
            rhs[k * 128 : (k + 1) * 128, 0:128] = block[0:128]
            tail = block[128:192].astype(F32)
            turned = pltpu.roll(tail, 64, 1)
            rhs[k * 128 : k * 128 + 64, 128:256] = jnp.where(lane64, tail, turned).astype(BF)
            rhs[k * 128 + 64 : (k + 1) * 128, 128:256] = jnp.where(lane64, turned, tail).astype(BF)
        row = jnp.concatenate(where, axis=1)
        for mine in (False, True):
            first = (core if mine else 1 - core) * 1024
            for m in range(2):
                hot = jnp.concatenate(
                    [one_hot(row, first + m * 256), one_hot(row, first + 512 + m * 256)], axis=0
                )
                total = dot(hot, rhs[...])
                tail = jnp.where(lanes < 64, total[0:256, 128:256], total[256:512, 128:256])
                ends = ((m * 256, total[0:256, 0:128]), (512 + m * 256, total[256:512, 0:128]), (1024 + m * 256, tail))
                for start, value in ends:
                    if mine:
                        own[i, start : start + 256, :] = value
                    else:
                        across[i, start : start + 256, :] = value.astype(BF)

    def pieces(i, p):
        at = slice(p * PIECE, (p + 1) * PIECE)
        return own[i, at, :] + across_in[i, at, :].astype(F32)

    for k in range(1, 8):
        index_copy(k).start()
    dense_1()

    def sort_step(i, carry):
        sort_chunk(i)
        for k in range(1, 8):
            lookup_copy(i, k).start()
        return carry

    lax.fori_loop(0, 2, sort_step, 0)
    dense_2()
    lax.fori_loop(2, 4, sort_step, 0)
    dense_3()
    lax.fori_loop(4, 8, sort_step, 0)
    for k in range(1, 8):
        index_copy(k).wait_recv()

    def add_step(i, carry):
        add_chunk(i)
        across_copy(i).start()
        return carry

    def ring_send(way, slot, value):
        ring_out[way, slot] = value.astype(BF)
        ring_copy(way, slot).start()

    def ring_got(way, slot):
        ring_copy(way, slot).wait_recv()
        return ring_in[way, slot].astype(F32)

    lax.fori_loop(0, 1, add_step, 0)
    across_copy(0).wait_recv()
    ring_send(0, 0, pieces(0, 0))
    ring_send(1, 0, pieces(0, 1))
    for level in range(3):
        lax.fori_loop(1 + 2 * level, 3 + 2 * level, add_step, 0)
        for i in (1 + 2 * level, 2 + 2 * level):
            across_copy(i).wait_recv()
        for slot in (1 + 2 * level, 2 + 2 * level):
            for way in range(2):
                value = pieces(1 + 2 * level + way, (slot + way) % 2)
                if slot >= 2:
                    value = value + ring_got(way, slot - 2)
                ring_send(way, slot, value)
        if level == 0:
            dense_4()
        elif level == 1:
            dense_5()
    lax.fori_loop(7, 8, add_step, 0)
    dense_6()
    across_copy(7).wait_recv()
    for p in (1, 0):
        total = pieces(7, p) + ring_got(0, 6 - p) + ring_got(1, 5 + p)
        finish[p] = total.astype(BF)
        chip_copy(p).start()
        core_copy(p).start()
    dense_7()
    for p in (1, 0):
        chip_copy(p).wait_recv()
        forward_copy(p).start()

    eye = iota((128, 128), 0) == iota((128, 128), 1)
    lane128 = iota((128, 128), 1) < 64

    def update(half, first, second):
        for m in range(8):
            def packed(ref, start):
                return ref[start // PIECE, start % PIECE : start % PIECE + 128, :].astype(F32)

            main = packed(first, m * 128) + packed(second, m * 128)
            at = 1024 + (m % 4) * 128
            tail = packed(first, at) + packed(second, at)
            if m >= 4:
                tail = pltpu.roll(tail, 64, 1)
            square = main * main + jnp.where(lane128, tail * tail, 0.0)
            mean = jnp.sum(square, axis=1, keepdims=True) * (1.0 / WIDTH)
            before = jnp.broadcast_to(accum_ref[pl.ds(half * 8 + m, 1), :], (128, 128))
            before = jnp.sum(jnp.where(eye, before, 0.0), axis=1, keepdims=True)
            after = before + mean
            shown = jnp.broadcast_to(after, (128, 128))
            new_accum_ref[pl.ds(half * 8 + m, 1), :] = jnp.sum(
                jnp.where(eye, shown, 0.0), axis=0, keepdims=True
            )
            rate = LEARN_RATE / jnp.sqrt(after)
            rows = pl.ds(pl.multiple_of(half * 1024 + m * 128, 128), 128)
            new_table_ref[rows, 0:128] = table_ref[rows, 0:128] - main * rate
            new_table_ref[rows, 128:192] = table_ref[rows, 128:192] - (tail * rate)[:, 0:64]

    update(core, finish, chip_in)
    for p in (1, 0):
        core_copy(p).wait_recv()
        forward_copy(p).wait_recv()
    update(1 - core, core_in, core_in2)
    dense_8()

    for k in range(1, 8):
        index_copy(k).wait_send()
        z_copy(k).wait_send()

    def sent(i, carry):
        for k in range(1, 8):
            lookup_copy(i, k).wait_send()
        across_copy(i).wait_send()
        return carry

    lax.fori_loop(0, 8, sent, 0)
    for way in range(2):
        for slot in range(7):
            ring_copy(way, slot).wait_send()
    for p in range(2):
        chip_copy(p).wait_send()
        core_copy(p).wait_send()
        forward_copy(p).wait_send()
    half_copy().wait_send()
    for k in (1, 2, 3):
        y_copy(k).wait_send()
        x_copy(k).wait_send()
        xg_copy(k).wait_send()
        yg_copy(k).wait_send()
    cg_copy().wait_send()


def exchange_call(key, local, rows, dense, table, accum):
    dma = pltpu.SemaphoreType.DMA
    vmem = pltpu.VMEM
    return pl.pallas_call(
        exchange_kernel,
        out_shape=(
            jax.ShapeDtypeStruct((2048, WIDTH), F32),
            jax.ShapeDtypeStruct((16, 128), F32),
            jax.ShapeDtypeStruct((256, 128), F32),
            jax.ShapeDtypeStruct((128, 192), F32),
            jax.ShapeDtypeStruct((256, 256), F32),
        ),
        in_specs=[VM] * 6,
        out_specs=(VM,) * 5,
        scratch_shapes=[
            vmem((8, 8, 192, 128), BF),
            vmem((8, 8, 192, 128), BF),
            vmem((8, 8, 128), jnp.int32),
            vmem((1024, 256), BF),
            vmem((8, PACK, 128), F32),
            vmem((8, PACK, 128), BF),
            vmem((8, PACK, 128), BF),
            vmem((2, 7, PIECE, 128), BF),
            vmem((2, 7, PIECE, 128), BF),
            vmem((2, PIECE, 128), BF),
            vmem((2, PIECE, 128), BF),
            vmem((2, PIECE, 128), BF),
            vmem((2, PIECE, 128), BF),
            vmem((4, 128, 128), F32),
            vmem((512, 128), F32),
            vmem((3, 128, 128), F32),
            vmem((4, 32, 128), F32),
            vmem((3, 32, 128), F32),
            vmem((8, 32, 128), F32),
            vmem((4, 32, 128), F32),
            vmem((4, 128, 128), F32),
            vmem((2, 512, 128), F32),
            dma((8, 8)), dma((8, 8)), dma((8,)), dma((8,)), dma((8,)), dma((8,)),
            dma((2, 7)), dma((2, 7)), dma((3, 2)), dma((3, 2)), dma((21,)), dma((21,)),
        ],
        compiler_params=pltpu.CompilerParams(
            collective_id=0, has_side_effects=True, vmem_limit_bytes=63 * 2**20
        ),
        name="exchange",
    )(key, local, rows, dense, table, accum)


def on_device(layer_input, out_grad, mix_weight, lift_weight, linear_weight, row_ids, row_home, table, row_accum):
    key, local = index_call(row_ids, row_home.reshape(1024, 128))
    rows, dense = layer_call(layer_input, out_grad, mix_weight, lift_weight, linear_weight)
    new_table, new_accum, mix_grad, lift_grad, linear_grad = exchange_call(
        key, local.reshape(8, 8, 128), rows, dense.reshape(2, 512, 128), table, row_accum.reshape(16, 128)
    )
    return (new_table, new_accum.reshape(-1), mix_grad, lift_grad, linear_grad)


def solution(mesh):
    placed = (
        P(("outer", "inner"), None, None),
        P(("outer", "inner"), None, None),
        P(), P(), P(),
        P(("outer", "inner"), None),
        P(),
        P("inner", None),
        P("inner"),
    )
    return jax.shard_map(
        on_device,
        mesh=mesh,
        in_specs=placed,
        out_specs=(P("inner", None), P("inner"), P(), P(), P()),
        check_vma=False,
    )
```

time: 613 us -> 160 us (0.26)
  waiting for transfers between devices: 300 us -> 0 us
  local copies, waits for them, and re-layouts: 218 us -> 26.1 us
  Pallas kernels: 0 us -> 131 us
  matrix products: 33.7 us -> 0 us
  starting transfers between devices: 26 us -> 0 us
  other arithmetic: 14.6 us -> 0 us
  between operations: 14.3 us -> 0.78 us
    psum x2 -> x0, waiting for transfers between devices: 240 us -> none  [the longest x1 188 us: on_device(): summed = lax.psum((totals[0], totals[1], totals[2]), ('outer', 'inner'))]
    gather x3 -> x0, local copies, waits for them, and re-layouts: 143 us -> none  [the longest x1 104 us: on_device(): placed = jnp.take(row_home, row_ids.reshape(-1), axis=0)]
    pallas_call x0 -> x3, Pallas kernels: none -> 131 us  [the longest x1 97.7 us: exchange_call(): pl.pallas_call(exchange_kernel, out_shape=(jax.ShapeDtypeStruct((2048, WI...]
    scatter x2 -> x0, local copies, waits for them, and re-layouts: 61.7 us -> none  [the longest x1 31 us: on_device(): local_rows = jnp.zeros((lookups,), jnp.int32).at[target].set(placed % tab...]
    all_to_all x2 -> x0, waiting for transfers between devices: 60.4 us -> none  [the longest x1 60.4 us: on_device(): lax.all_to_all(outgoing, 'inner', split_axis=0, concat_axis=0, tiled=True)]
    dot_general x14 -> x0, matrix products: 33.7 us -> none  [the longest x4 15.2 us: add_rows(): jnp.einsum('lr,ld->rd', hot, values[start:start + width], preferred_eleme...]
    all_to_all x2 -> x0, starting transfers between devices: 25.7 us -> none  [the longest x1 13.3 us: on_device(): lax.all_to_all(local_rows, 'inner', split_axis=0, concat_axis=0, tiled=True)]
    unnamed x22 -> x45, local copies, waits for them, and re-layouts: 5.39 us -> 26.1 us
  transfers between devices with their start and end apart: 4 -> 0, of which waited for: 3 -> 0; matrix products, arithmetic and copies ran while one was open for 20% -> 0% of each run, Pallas kernels for 0% -> 0%
where the time goes in v1:
time: 160 us; the launch traced here: 158 us
  Pallas kernels  131 us (82%)
  local copies, waits for them, and re-layouts  26.1 us (16%)
    pallas_call x1, Pallas kernels, exchange_call(): pl.pallas_call(exchange_kernel, out_shape=(jax.ShapeDtypeStruct((2048, WI...  97.7 us
    unnamed x45, local copies, waits for them, and re-layouts  26.1 us
    pallas_call x1, Pallas kernels, layer_call(): pl.pallas_call(layer_kernel, grid=(SAMPLES,), out_shape=(jax.ShapeDtypeSt...  20.6 us
    pallas_call x1, Pallas kernels, index_call(): pl.pallas_call(index_kernel, out_shape=(jax.ShapeDtypeStruct((SAMPLES, FE...  13.2 us

profile of v1, /device:TPU:15, one launch (start us, length us, event | category | flops | bytes accessed | tf_op | source)
XLA Modules:
  0.0 158.4 jit_solution(9020190290843431131)
XLA Ops:
  0.6 0.0 copy-start.10
  0.6 6.3 %copy.16.x_ref = bf16[32,256,192]{2,1,0:T(8,128)(2,1)} copy(bf16[32,256,192]{1,2,0:T(8,128)(2,1)} %param.9) | data formatting | bytes 6291456 | tf_op args[0]
  6.9 0.0 copy-done.10
  6.9 0.0 copy-start.14
  6.9 0.0 copy-start.5
  6.9 0.0 copy-start.6
  7.0 4.6 %copy.17.g_ref = bf16[32,256,192]{2,1,0:T(8,128)(2,1)} copy(bf16[32,256,192]{1,2,0:T(8,128)(2,1)S(1)} %copy-done.10) | data formatting | bytes 6291456 | tf_op args[1]
  11.6 0.0 copy-done.14
  11.6 0.1 copy.15
  11.7 0.0 copy-done.5
  11.7 0.1 copy.14
  11.8 0.0 copy-done.6
  11.8 0.1 copy.18.lift_ref
  11.9 0.0 copy-start
  11.9 2.2 %copy-done = bf16[32,256,192]{2,1,0:T(8,128)(2,1)S(1)} copy-done((bf16[32,256,192]{2,1,0:T(8,128)(2,1)S(1)}, bf16[32,256,192]{2,1,0:T(8,128)(2,1)}, u32[]{:S(2)}) %copy-start) | copy-done | bytes 3145752
  14.1 0.0 copy-start.1
  14.1 2.2 %copy-done.1 = bf16[32,256,192]{2,1,0:T(8,128)(2,1)S(1)} copy-done((bf16[32,256,192]{2,1,0:T(8,128)(2,1)S(1)}, bf16[32,256,192]{2,1,0:T(8,128)(2,1)}, u32[]{:S(2)}) %copy-start.1) | copy-done | bytes 3145752
  16.3 0.0 copy-start.3
  16.3 0.0 copy-start.9
  16.3 0.0 copy-start.11
  16.3 20.6 %layer.1 = (bf16[8192,256]{1,0:T(8,128)(2,1)S(1)}, f32[1024,128]{1,0:T(8,128)S(1)}) custom-call(bf16[32,256,192]{2,1,0:T(8,128)(2,1)S(1)} %copy-done, bf16[32,256,192]{2,1,0:T(8,128)(2,1)S(1)} %copy-done.1, bf16[256,128]{1,0:T(8,128)(2,1)S(1)} %copy-done.5, bf16[128,256]{1,0:T(8,128)(2,1)S(1)} %bitcast.11, bf16[128,192]{1,0:T(8,128)(2,1)S(1)} %copy.18.lift_ref, ...), custom_call_target="tpu_custom_call" | custom-call | tf_op jit(solution)/shard_map/layer/pallas_call | solution.py:127
  36.9 0.0 copy-start.2
  36.9 1.9 %copy-done.2 = bf16[8192,256]{1,0:T(8,128)(2,1)} copy-done((bf16[8192,256]{1,0:T(8,128)(2,1)}, bf16[8192,256]{1,0:T(8,128)(2,1)S(1)}, u32[]{:S(2)}) %copy-start.2) | copy-done | bytes 4194328
  38.8 0.0 copy-start.4
  38.8 0.0 copy-done.3
  38.8 0.0 copy-done.9
  38.8 13.2 %index.1 = (s32[32,256]{1,0:T(8,128)S(1)}, s32[64,128]{1,0:T(8,128)S(1)}) custom-call(s32[32,256]{1,0:T(8,128)S(1)} %copy-done.9, s32[1024,128]{1,0:T(8,128)S(1)} %bitcast.9), custom_call_target="tpu_custom_call" | custom-call | tf_op jit(solution)/shard_map/index/pallas_call | solution.py:83
  52.0 0.0 copy-done.4
  52.0 0.0 copy-start.7
  52.1 0.6 copy-done.7
  52.7 0.0 copy-start.8
  52.7 0.6 copy-done.8
  53.3 0.0 copy-done.11
  53.3 1.8 %copy.19.table_ref = f32[2048,192]{1,0:T(8,128)} copy(f32[2048,192]{0,1:T(8,128)S(1)} %copy-done.11) | data formatting | bytes 3145728 | tf_op args[7]
  55.1 97.7 %exchange.1 = (f32[2048,192]{1,0:T(8,128)}, f32[16,128]{1,0:T(8,128)}, f32[256,128]{1,0:T(8,128)}, f32[128,192]{1,0:T(8,128)}, f32[256,256]{1,0:T(8,128)}) custom-call(s32[32,256]{1,0:T(8,128)} %copy-done.7, s32[8,8,128]{2,1,0:T(8,128)} %bitcast.13, bf16[8192,256]{1,0:T(8,128)(2,1)} %copy-done.2, f32[2,512,128]{2,1,0:T(8,128)} %bitcast.10, ...), custom_call_target="tpu_custom_call" | custom-call | tf_op jit(solution)/shard_map/exchange/pallas_call | solution.py:531
  152.8 0.0 copy-start.13
  152.8 0.0 copy-start.16
  152.9 0.0 copy-start.15
  152.9 0.0 copy-start.12
  152.9 2.8 %copy.20 = f32[2048,192]{0,1:T(8,128)} copy(f32[2048,192]{1,0:T(8,128)} %get-tuple-element.23) | data formatting | bytes 3145728
  155.7 0.0 copy-done.13
  155.7 0.7 copy.21
  156.5 0.0 copy-done.16
  156.5 0.6 copy.25
  157.1 0.0 copy-done.15
  157.1 0.7 copy.26
  157.7 0.0 copy-done.12
  157.7 0.7 copy.27
Async XLA Ops:
  0.6 6.3 %copy-start.10 = (bf16[32,256,192]{1,2,0:T(8,128)(2,1)S(1)}, bf16[32,256,192]{1,2,0:T(8,128)(2,1)}, u32[]{:S(2)}) copy-start(bf16[32,256,192]{1,2,0:T(8,128)(2,1)} %param.10) | copy-start | bytes 9437188
  6.9 4.6 %copy-start.14 = (bf16[256,256]{1,0:T(8,128)(2,1)S(1)}, bf16[256,256]{1,0:T(8,128)(2,1)}, u32[]{:S(2)}) copy-start(bf16[256,256]{1,0:T(8,128)(2,1)} %param.13) | copy-start | bytes 393220
  6.9 4.7 %copy-start.5 = (bf16[256,128]{1,0:T(8,128)(2,1)S(1)}, bf16[256,128]{1,0:T(8,128)(2,1)}, u32[]{:S(2)}) copy-start(bf16[256,128]{1,0:T(8,128)(2,1)} %mix_ref.1) | copy-start | bytes 196612
  6.9 4.8 %copy-start.6 = (bf16[128,192]{0,1:T(8,128)(2,1)S(1)}, bf16[128,192]{0,1:T(8,128)(2,1)}, u32[]{:S(2)}) copy-start(bf16[128,192]{0,1:T(8,128)(2,1)} %param.12) | copy-start | bytes 147460
  11.9 2.2 %copy-start = (bf16[32,256,192]{2,1,0:T(8,128)(2,1)S(1)}, bf16[32,256,192]{2,1,0:T(8,128)(2,1)}, u32[]{:S(2)}) copy-start(bf16[32,256,192]{2,1,0:T(8,128)(2,1)} %copy.16.x_ref) | copy-start | bytes 9437188
  14.1 2.2 %copy-start.1 = (bf16[32,256,192]{2,1,0:T(8,128)(2,1)S(1)}, bf16[32,256,192]{2,1,0:T(8,128)(2,1)}, u32[]{:S(2)}) copy-start(bf16[32,256,192]{2,1,0:T(8,128)(2,1)} %copy.17.g_ref) | copy-start | bytes 9437188
  16.3 22.5 %copy-start.3 = (s32[131072]{0:T(1024)S(1)}, s32[131072]{0:T(1024)}, u32[]{:S(2)}) copy-start(s32[131072]{0:T(1024)} %param.15) | copy-start | bytes 1572868
  16.3 22.5 %copy-start.9 = (s32[32,256]{1,0:T(8,128)S(1)}, s32[32,256]{1,0:T(8,128)}, u32[]{:S(2)}) copy-start(s32[32,256]{1,0:T(8,128)} %ids_ref.1) | copy-start | bytes 98308
  16.3 37.0 %copy-start.11 = (f32[2048,192]{0,1:T(8,128)S(1)}, f32[2048,192]{0,1:T(8,128)}, u32[]{:S(2)}) copy-start(f32[2048,192]{0,1:T(8,128)} %param.16) | copy-start | bytes 4718596
  36.9 2.0 %copy-start.2 = (bf16[8192,256]{1,0:T(8,128)(2,1)}, bf16[8192,256]{1,0:T(8,128)(2,1)S(1)}, u32[]{:S(2)}) copy-start(bf16[8192,256]{1,0:T(8,128)(2,1)S(1)} %get-tuple-element.16.rows_ref) | copy-start | bytes 12582916
  38.8 13.2 %copy-start.4 = (f32[1024,128]{1,0:T(8,128)}, f32[1024,128]{1,0:T(8,128)S(1)}, u32[]{:S(2)}) copy-start(f32[1024,128]{1,0:T(8,128)S(1)} %get-tuple-element.17) | copy-start | bytes 1572868
  52.0 0.6 copy-start.7
  52.7 0.6 copy-start.8
  152.8 2.9 %copy-start.13 = (f32[128,192]{1,0:T(8,128)S(1)}, f32[128,192]{1,0:T(8,128)}, u32[]{:S(2)}) copy-start(f32[128,192]{1,0:T(8,128)} %get-tuple-element.26) | copy-start | bytes 294916
  152.8 3.6 %copy-start.16 = (f32[16,128]{1,0:T(8,128)S(1)}, f32[16,128]{1,0:T(8,128)}, u32[]{:S(2)}) copy-start(f32[16,128]{1,0:T(8,128)} %get-tuple-element.19) | copy-start | bytes 24580
  152.9 4.2 %copy-start.15 = (f32[256,128]{1,0:T(8,128)S(1)}, f32[256,128]{1,0:T(8,128)}, u32[]{:S(2)}) copy-start(f32[256,128]{1,0:T(8,128)} %get-tuple-element.35) | copy-start | bytes 393220
  152.9 4.9 %copy-start.12 = (f32[256,256]{1,0:T(8,128)S(1)}, f32[256,256]{1,0:T(8,128)}, u32[]{:S(2)}) copy-start(f32[256,256]{1,0:T(8,128)} %get-tuple-element.37) | copy-start | bytes 786436

commit v2 on v1

v2 whole, which is shorter than its diff:
```python
import math

import jax
import jax.numpy as jnp
from jax import lax
from jax.experimental import pallas as pl
from jax.experimental.pallas import tpu as pltpu
from jax.sharding import PartitionSpec as P

LEARN_RATE = 0.5
MESH = pl.DeviceIdType.MESH
BF = jnp.bfloat16
F32 = jnp.float32
VM = pl.BlockSpec(memory_space=pltpu.VMEM)

SAMPLES, FEATS, WIDTH, RANK = 32, 256, 192, 128
BATCH = 8192
HALF = 4096
PIECE = 512
TOGETHER = 4


def dot(a, b, dims=((1,), (0,))):
    return lax.dot_general(a, b, (dims, ((), ())), preferred_element_type=F32)


NT = ((1,), (1,))


def iota(shape, axis):
    return lax.broadcasted_iota(jnp.int32, shape, axis)


def one_hot(rows, row, base):
    near = (row - base).astype(F32).astype(BF)
    tiles = []
    for t in range(row.shape[1] // 128):
        part = jnp.broadcast_to(near[:, t * 128 : (t + 1) * 128], (256, 128))
        tiles.append(jnp.where(rows == part, jnp.ones((), BF), jnp.zeros((), BF)))
    return jnp.concatenate(tiles, axis=1)


def index_kernel(ids_ref, home_ref, key_ref, local_ref, table_t, place_ref):
    home = home_ref[...]
    high = (home >> 9).astype(F32)
    low = ((home & 511) - 256).astype(F32)
    table_t[0:128, :] = high.T.astype(BF)
    table_t[128:256, :] = low.T.astype(BF)
    rows256 = iota((256, 128), 0).astype(F32).astype(BF)
    rows128 = iota((128, 256), 0)

    def look(b, carry):
        ids = ids_ref[pl.ds(b, 1), :]
        high_id = ids >> 7
        hot = jnp.concatenate([one_hot(rows256, high_id, base) for base in (0, 256, 512, 768)], axis=0)
        found = dot(table_t[...], hot)
        mask = rows128 == (ids & 127)
        high_part = jnp.sum(jnp.where(mask, found[0:128], 0.0), axis=0, keepdims=True)
        low_part = jnp.sum(jnp.where(mask, found[128:256], 0.0), axis=0, keepdims=True)
        place_ref[pl.ds(b, 1), :] = (high_part * 512.0 + low_part + 256.0).astype(jnp.int32)
        return carry

    lax.fori_loop(0, SAMPLES, look, 0, unroll=4)
    upper = (iota((256, 256), 0) < iota((256, 256), 1)).astype(F32).astype(BF)
    rows64 = iota((64, 256), 0)
    for half in range(2):

        def rank(step, carry):
            counts, firsts = carry
            b = half * 16 + step
            place = place_ref[pl.ds(b, 1), :]
            owner = place >> 11
            local = place & 2047
            own = (rows64 == owner).astype(F32)
            before = dot(own.astype(BF), upper) + counts
            rank_of = jnp.sum(own * before, axis=0, keepdims=True).astype(jnp.int32)
            key_ref[pl.ds(b, 1), :] = (owner & 7) * 512 + (owner >> 3) * 64 + rank_of
            hot = (rows64 == rank_of).astype(F32).astype(BF)
            parts = jnp.concatenate(
                [own * (local >> 4).astype(F32), own * (local & 15).astype(F32)], axis=0
            ).astype(BF)
            firsts = firsts + dot(parts, hot, NT)
            counts = counts + jnp.sum(own, axis=1, keepdims=True)
            return counts, firsts

        start = (jnp.zeros((64, 1), F32), jnp.zeros((128, 64), F32))
        unused, firsts = lax.fori_loop(0, 16, rank, start, unroll=16)
        merged = firsts[0:64] * 16.0 + firsts[64:128]
        local_ref[:, half * 64 : (half + 1) * 64] = merged.astype(jnp.int32)


def index_call(row_ids, home):
    return pl.pallas_call(
        index_kernel,
        out_shape=(
            jax.ShapeDtypeStruct((SAMPLES, FEATS), jnp.int32),
            jax.ShapeDtypeStruct((64, 128), jnp.int32),
        ),
        in_specs=[VM, VM],
        out_specs=(VM, VM),
        scratch_shapes=[pltpu.VMEM((256, 1024), BF), pltpu.VMEM((SAMPLES, FEATS), jnp.int32)],
        compiler_params=pltpu.CompilerParams(vmem_limit_bytes=63 * 2**20),
        name="index",
    )(row_ids, home)


def layer_kernel(xt_ref, gt_ref, mix_ref, lift_t_ref, linear_ref, rows_ref, dense_ref, left_ref, linear_mix_ref, lift_ref):
    scaling = 1.0 / math.sqrt(WIDTH)

    @pl.when(pl.program_id(0) == 0)
    def _():
        dense_ref[...] = jnp.zeros_like(dense_ref)
        left_ref[...] = mix_ref[...].astype(F32).T.astype(BF)
        lift_ref[...] = lift_t_ref[...].astype(F32).T.astype(BF)
        linear_mix_ref[:, 0:256] = linear_ref[...].astype(F32).T.astype(BF)
        linear_mix_ref[:, 256:384] = mix_ref[...]

    for n in range(TOGETHER):
        xt = xt_ref[n]
        gt = gt_ref[n]
        g = gt.T
        d_products_t = dot(lift_ref[...], gt).astype(BF)
        both = dot(jnp.concatenate([left_ref[...], d_products_t], axis=0), xt, NT)
        compressed_t = both[0:128].astype(BF)
        d_compressed_t = (both[128:256] * scaling).astype(BF)
        next_both = dot(jnp.concatenate([compressed_t, d_compressed_t], axis=0), xt)
        products_t = (next_both[0:128] * scaling).astype(BF)
        d_inputs = g.astype(F32) + dot(
            linear_mix_ref[...], jnp.concatenate([g, d_compressed_t], axis=0)
        )
        d_inputs = d_inputs + scaling * dot(d_products_t.T, compressed_t)
        rows_ref[n * FEATS : (n + 1) * FEATS, :] = d_inputs.astype(BF)
        dense_ref[0:128] += next_both[128:256, 0:128]
        dense_ref[128:256] += next_both[128:256, 128:256]
        linear = dot(g, xt)
        dense_ref[256:512] += linear[:, 0:128]
        dense_ref[512:768] += linear[:, 128:256]
        dense_ref[768:960] += dot(gt, products_t, NT)


def layer_call(xt, gt, mix, lift_t, linear):
    whole = lambda shape: pl.BlockSpec(shape, lambda b: (0, 0))
    return pl.pallas_call(
        layer_kernel,
        grid=(SAMPLES // TOGETHER,),
        out_shape=(
            jax.ShapeDtypeStruct((SAMPLES * FEATS, WIDTH), BF),
            jax.ShapeDtypeStruct((1024, 128), F32),
        ),
        in_specs=[
            pl.BlockSpec((TOGETHER, WIDTH, FEATS), lambda b: (b, 0, 0)),
            pl.BlockSpec((TOGETHER, WIDTH, FEATS), lambda b: (b, 0, 0)),
            whole((256, 128)),
            whole((192, 128)),
            whole((256, 256)),
        ],
        out_specs=(pl.BlockSpec((TOGETHER * FEATS, WIDTH), lambda b: (b, 0)), whole((1024, 128))),
        scratch_shapes=[
            pltpu.VMEM((128, 256), BF), pltpu.VMEM((256, 384), BF), pltpu.VMEM((128, 192), BF),
        ],
        compiler_params=pltpu.CompilerParams(
            vmem_limit_bytes=63 * 2**20, dimension_semantics=("arbitrary",)
        ),
        name="layer",
    )(xt, gt, mix, lift_t, linear)


class Spot:
    def __init__(self):
        outer = lax.axis_index("outer")
        inner = lax.axis_index("inner")
        self.core = lax.rem(outer, 2)
        self.y_lo = outer // 2
        self.x = inner // 16
        self.y_hi = lax.rem(inner // 8, 2)
        self.z = lax.rem(inner, 8)
        self.y = self.y_hi * 2 + self.y_lo

    def at(self, x=None, y=None, z=None, core=None):
        x = self.x if x is None else x
        y = self.y if y is None else y
        z = self.z if z is None else z
        core = self.core if core is None else core
        return (lax.rem(y, 2) * 2 + core, (x * 2 + y // 2) * 8 + z)


def chunk_offset(i):
    return 4 + (1 - 2 * (i % 2)) * ((i + 1) // 2)


def exchange_kernel(
    key_ref, local_ref, rows_any, dense_ref,
    near, far, d_cg,
    rows_ref, send, recv, local_in, own, across, across_in, ring_out, ring_in,
    d_half, d_half_in, d_y_in, d_y, d_x_in, d_z, d_xg, d_yg,
    s_send, s_recv, i_send, i_recv, a_send, a_recv, r_send, r_recv, f_send, f_recv, d_send, d_recv, in_sem,
):
    me = Spot()
    x, y, z, core = me.x, me.y, me.z, me.core
    iota_rows = iota((256, 128), 0).astype(F32).astype(BF)

    def peer(k):
        dx, dy = k // 2, k % 2
        y_to = me.y if dy == 0 else (1 - me.y_hi) * 2 + (1 - me.y_lo)
        return me.at(x=lax.rem(x + dx, 4), y=y_to)

    def place_of(k):
        dx, dy = k // 2, k % 2
        return lax.rem(x + dx, 4) * 2 + (me.y_hi if dy == 0 else 1 - me.y_hi)

    partner = me.at(core=1 - core)
    beside = me.at(y=me.y_hi * 2 + 1 - me.y_lo)
    up = me.at(z=lax.rem(z + 1, 8))
    down = me.at(z=lax.rem(z + 7, 8))
    y_peer = lambda k: me.at(y=lax.rem(y + k, 4))
    x_peer = lambda k: me.at(x=lax.rem(x + k, 4))
    z_peer = lambda k: me.at(z=lax.rem(z + k, 8))

    barrier = pltpu.get_barrier_semaphore()
    greeted = (
        [peer(k) for k in range(1, 8)]
        + [partner]
        + [y_peer(k) for k in (1, 2, 3)]
        + [x_peer(k) for k in (1, 2, 3)]
        + [z_peer(k) for k in range(1, 8)]
    )
    load = pltpu.make_async_copy(rows_any, rows_ref, in_sem)
    load.start()
    for device in greeted:
        pl.semaphore_signal(barrier, inc=1, device_id=device, device_id_type=MESH)
    pl.semaphore_wait(barrier, len(greeted))
    load.wait()

    def copy(src, dst, send_sem, recv_sem, device):
        return pltpu.make_async_remote_copy(
            src_ref=src, dst_ref=dst, send_sem=send_sem, recv_sem=recv_sem,
            device_id=device, device_id_type=MESH,
        )

    def index_copy(k):
        return copy(local_ref.at[place_of(k)], local_in.at[k], i_send.at[k], i_recv.at[k], peer(k))

    def lookup_copy(i, k):
        return copy(send.at[i, place_of(k)], recv.at[i, k], s_send.at[i, k], s_recv.at[i, k], peer(k))

    def across_copy(i):
        return copy(across.at[i], across_in.at[i], a_send.at[i], a_recv.at[i], partner)

    def ring_copy(way, slot):
        return copy(
            ring_out.at[way, slot], ring_in.at[way, slot], r_send.at[way, slot], r_recv.at[way, slot],
            (up, down)[way],
        )

    def chip_copy(p):
        return copy(near.at[core, p], far.at[core, p], f_send.at[0, p], f_recv.at[0, p], beside)

    def core_copy(p):
        return copy(near.at[core, p], near.at[core, p], f_send.at[1, p], f_recv.at[1, p], partner)

    def core_wait(p):
        return copy(near.at[core, p], near.at[1 - core, p], f_send.at[1, p], f_recv.at[1, p], partner)

    def forward_copy(p):
        return copy(far.at[core, p], far.at[core, p], f_send.at[2, p], f_recv.at[2, p], partner)

    def forward_wait(p):
        return copy(far.at[core, p], far.at[1 - core, p], f_send.at[2, p], f_recv.at[2, p], partner)

    def half_copy():
        return copy(dense_ref.at[1 - core], d_half_in, d_send.at[0], d_recv.at[0], partner)

    def y_copy(k):
        return copy(d_half.at[lax.rem(y + k, 4)], d_y_in.at[k - 1], d_send.at[k], d_recv.at[k], y_peer(k))

    def x_copy(k):
        return copy(d_y.at[lax.rem(x + k, 4)], d_x_in.at[k - 1], d_send.at[3 + k], d_recv.at[3 + k], x_peer(k))

    def z_copy(k):
        return copy(d_z.at[z], d_z.at[z], d_send.at[6 + k], d_recv.at[6 + k], z_peer(k))

    def z_wait(k):
        return copy(d_z.at[z], d_z.at[lax.rem(z + 8 - k, 8)], d_send.at[6 + k], d_recv.at[6 + k], z_peer(k))

    def xg_copy(k):
        return copy(d_xg.at[x], d_xg.at[x], d_send.at[13 + k], d_recv.at[13 + k], x_peer(k))

    def xg_wait(k):
        return copy(d_xg.at[x], d_xg.at[lax.rem(x + 4 - k, 4)], d_send.at[13 + k], d_recv.at[13 + k], x_peer(k))

    def yg_copy(k):
        return copy(d_yg.at[y], d_yg.at[y], d_send.at[16 + k], d_recv.at[16 + k], y_peer(k))

    def yg_wait(k):
        return copy(d_yg.at[y], d_yg.at[lax.rem(y + 4 - k, 4)], d_send.at[16 + k], d_recv.at[16 + k], y_peer(k))

    def cg_copy():
        return copy(d_cg.at[core], d_cg.at[core], d_send.at[20], d_recv.at[20], partner)

    def cg_wait():
        return copy(d_cg.at[core], d_cg.at[1 - core], d_send.at[20], d_recv.at[20], partner)

    def dense_1():
        half_copy().start()

    def dense_2():
        half_copy().wait_recv()
        total = dense_ref[core] + d_half_in[...]
        d_half[...] = total.reshape(4, 128, 128)
        for k in (1, 2, 3):
            y_copy(k).start()

    def dense_3():
        for k in (1, 2, 3):
            y_copy(k).wait_recv()
        total = d_half[y] + d_y_in[0] + d_y_in[1] + d_y_in[2]
        d_y[...] = total.reshape(4, 32, 128)
        for k in (1, 2, 3):
            x_copy(k).start()

    def dense_4():
        for k in (1, 2, 3):
            x_copy(k).wait_recv()
        d_z[z] = d_y[x] + d_x_in[0] + d_x_in[1] + d_x_in[2]
        for k in range(1, 8):
            z_copy(k).start()

    def dense_5():
        for k in range(1, 8):
            z_wait(k).wait_recv()
        total = d_z[0]
        for k in range(1, 8):
            total = total + d_z[k]
        d_xg[x] = total * (1.0 / BATCH)
        for k in (1, 2, 3):
            xg_copy(k).start()

    def dense_6():
        for k in (1, 2, 3):
            xg_wait(k).wait_recv()
        d_yg[y] = d_xg[...].reshape(128, 128)
        for k in (1, 2, 3):
            yg_copy(k).start()

    def dense_7():
        for k in (1, 2, 3):
            yg_wait(k).wait_recv()
        d_cg[core] = d_yg[...].reshape(512, 128)
        cg_copy().start()

    def dense_8():
        cg_wait().wait_recv()

    def sort_chunk(i):
        to = lax.rem(z + chunk_offset(i), 8)
        got = []
        for half in range(2):
            total = jnp.zeros((512, WIDTH), F32)
            for t in range(4):
                hot = []
                for part in range(2):
                    base = to * 512 + part * 256
                    tiles = [
                        one_hot(iota_rows, key_ref[pl.ds(half * 16 + t * 4 + b, 1), :], base) for b in range(4)
                    ]
                    hot.append(jnp.concatenate(tiles, axis=1))
                start = half * HALF + t * 1024
                total = total + dot(jnp.concatenate(hot, axis=0), rows_ref[start : start + 1024, :])
            got.append(total)
        for q in range(8):
            at = slice(q * 64, (q + 1) * 64)
            block = jnp.concatenate([got[0][at], got[1][at]], axis=0)
            send[i, q] = block.T.astype(BF)

    def add_chunk(i):
        to = lax.rem(z + chunk_offset(i), 8)
        where = []
        blocks = []
        for k in range(8):
            if k == 0:
                blocks.append(send[i, place_of(0)])
                where.append(local_ref[place_of(0), pl.ds(to, 1), :])
            else:
                lookup_copy(i, k).wait_recv()
                blocks.append(recv[i, k])
                where.append(local_in[k, pl.ds(to, 1), :])
        block = jnp.concatenate(blocks, axis=1)
        row = jnp.concatenate(where, axis=1)
        for mine in (False, True):
            first = (core if mine else 1 - core) * 1024
            for m in range(4):
                total = dot(block, one_hot(iota_rows, row, first + m * 256), NT)
                at = slice(m * 256, (m + 1) * 256)
                if mine:
                    own[i, :, at] = total
                else:
                    across[i, :, at] = total.astype(BF)
            if not mine:
                across_copy(i).start()

    def pieces(i, p):
        at = slice(p * PIECE, (p + 1) * PIECE)
        return own[i, :, at] + across_in[i, :, at].astype(F32)

    for k in range(1, 8):
        index_copy(k).start()
    dense_1()

    def sort_step(i, carry):
        sort_chunk(i)
        for k in range(1, 8):
            lookup_copy(i, k).start()
        return carry

    def add_step(i, carry):
        add_chunk(i)
        return carry

    def ring_send(way, slot, value):
        ring_out[way, slot] = value.astype(BF)
        ring_copy(way, slot).start()

    def ring_got(way, slot):
        ring_copy(way, slot).wait_recv()
        return ring_in[way, slot].astype(F32)

    def ring_level(way, level):
        i = 1 + 2 * level + way
        across_copy(i).wait_recv()
        for slot in (1 + 2 * level, 2 + 2 * level):
            value = pieces(i, (slot + way) % 2)
            if slot >= 2:
                value = value + ring_got(way, slot - 2)
            ring_send(way, slot, value)

    def sorts(first, last):
        lax.fori_loop(first, last, sort_step, 0)

    def adds(first, last):
        lax.fori_loop(first, last, add_step, 0)

    sorts(0, 1)
    dense_2()
    sorts(1, 4)
    for k in range(1, 8):
        index_copy(k).wait_recv()
    adds(0, 1)
    dense_3()
    adds(1, 2)
    across_copy(0).wait_recv()
    ring_send(0, 0, pieces(0, 0))
    ring_send(1, 0, pieces(0, 1))
    sorts(4, 5)
    ring_level(0, 0)
    adds(2, 3)
    sorts(5, 6)
    ring_level(1, 0)
    dense_4()
    adds(3, 4)
    sorts(6, 7)
    ring_level(0, 1)
    adds(4, 5)
    sorts(7, 8)
    ring_level(1, 1)
    dense_5()
    adds(5, 6)
    ring_level(0, 2)
    adds(6, 7)
    ring_level(1, 2)
    dense_6()
    adds(7, 8)
    dense_7()
    across_copy(7).wait_recv()
    for p in (1, 0):
        total = pieces(7, p) + ring_got(0, 6 - p) + ring_got(1, 5 + p)
        near[core, p] = total.astype(BF)
        chip_copy(p).start()
        core_copy(p).start()
    for p in (1, 0):
        chip_copy(p).wait_recv()
        forward_copy(p).start()
    dense_8()
    for p in (1, 0):
        core_wait(p).wait_recv()
        forward_wait(p).wait_recv()

    for k in range(1, 8):
        index_copy(k).wait_send()
        z_copy(k).wait_send()

    def sent(i, carry):
        for k in range(1, 8):
            lookup_copy(i, k).wait_send()
        across_copy(i).wait_send()
        return carry

    lax.fori_loop(0, 8, sent, 0)
    for way in range(2):
        for slot in range(7):
            ring_copy(way, slot).wait_send()
    for p in range(2):
        chip_copy(p).wait_send()
        core_copy(p).wait_send()
        forward_copy(p).wait_send()
    half_copy().wait_send()
    for k in (1, 2, 3):
        y_copy(k).wait_send()
        x_copy(k).wait_send()
        xg_copy(k).wait_send()
        yg_copy(k).wait_send()
    cg_copy().wait_send()


def exchange_call(key, local, rows, dense):
    dma = pltpu.SemaphoreType.DMA
    vmem = pltpu.VMEM
    return pl.pallas_call(
        exchange_kernel,
        out_shape=(
            jax.ShapeDtypeStruct((2, 2, WIDTH, PIECE), BF),
            jax.ShapeDtypeStruct((2, 2, WIDTH, PIECE), BF),
            jax.ShapeDtypeStruct((2, 512, 128), F32),
        ),
        in_specs=[VM, VM, pl.BlockSpec(memory_space=pl.ANY), VM],
        out_specs=(VM,) * 3,
        scratch_shapes=[
            vmem((SAMPLES * FEATS, WIDTH), BF),
            vmem((8, 8, 192, 128), BF),
            vmem((8, 8, 192, 128), BF),
            vmem((8, 8, 128), jnp.int32),
            vmem((8, WIDTH, 1024), F32),
            vmem((8, WIDTH, 1024), BF),
            vmem((8, WIDTH, 1024), BF),
            vmem((2, 7, WIDTH, PIECE), BF),
            vmem((2, 7, WIDTH, PIECE), BF),
            vmem((4, 128, 128), F32),
            vmem((512, 128), F32),
            vmem((3, 128, 128), F32),
            vmem((4, 32, 128), F32),
            vmem((3, 32, 128), F32),
            vmem((8, 32, 128), F32),
            vmem((4, 32, 128), F32),
            vmem((4, 128, 128), F32),
            dma((8, 8)), dma((8, 8)), dma((8,)), dma((8,)), dma((8,)), dma((8,)),
            dma((2, 7)), dma((2, 7)), dma((3, 2)), dma((3, 2)), dma((21,)), dma((21,)), dma(()),
        ],
        compiler_params=pltpu.CompilerParams(
            collective_id=0, has_side_effects=True, vmem_limit_bytes=60 * 2**20
        ),
        name="exchange",
    )(key, local, rows, dense)


def update_kernel(near_ref, far_ref, dense_ref, table_ref, accum_ref, new_table_ref, new_accum_ref, mix_ref, lift_ref, linear_ref):
    step = pl.program_id(0)
    for q in range(4):
        block = slice(q * 128, (q + 1) * 128)
        total = near_ref[0, :, block].astype(F32) + far_ref[0, :, block].astype(F32)
        mean = jnp.sum(total * total, axis=0, keepdims=True) * (1.0 / WIDTH)
        after = accum_ref[pl.ds(step * 4 + q, 1), :] + mean
        new_accum_ref[pl.ds(step * 4 + q, 1), :] = after
        rate = LEARN_RATE / jnp.sqrt(after)
        new_table_ref[:, block] = table_ref[:, block] - total * rate

    @pl.when(step == 0)
    def _():
        mix_ref[0:128, :] = dense_ref[0, 0:128].T
        mix_ref[128:256, :] = dense_ref[0, 128:256].T
        linear_ref[:, 0:128] = dense_ref[0, 256:512]
        linear_ref[:, 128:256] = dense_ref[1, 0:256]
        lift_ref[...] = dense_ref[1, 256:448]


def update_call(near, far, dense, table, accum):
    whole = lambda *shape: pl.BlockSpec(shape, lambda i: (0,) * len(shape))
    columns = pl.BlockSpec((WIDTH, PIECE), lambda i: (0, i))
    return pl.pallas_call(
        update_kernel,
        grid=(4,),
        out_shape=(
            jax.ShapeDtypeStruct((WIDTH, 2048), F32),
            jax.ShapeDtypeStruct((16, 128), F32),
            jax.ShapeDtypeStruct((256, 128), F32),
            jax.ShapeDtypeStruct((192, 128), F32),
            jax.ShapeDtypeStruct((256, 256), F32),
        ),
        in_specs=[
            pl.BlockSpec((1, WIDTH, PIECE), lambda i: (i, 0, 0)),
            pl.BlockSpec((1, WIDTH, PIECE), lambda i: (i, 0, 0)),
            whole(2, 512, 128),
            columns,
            whole(16, 128),
        ],
        out_specs=(columns, whole(16, 128), whole(256, 128), whole(192, 128), whole(256, 256)),
        compiler_params=pltpu.CompilerParams(
            vmem_limit_bytes=63 * 2**20, dimension_semantics=("arbitrary",)
        ),
        name="update",
    )(near.reshape(4, WIDTH, PIECE), far.reshape(4, WIDTH, PIECE), dense, table, accum)


def on_device(layer_input, out_grad, mix_weight, lift_weight, linear_weight, row_ids, row_home, table, row_accum):
    key, local = index_call(row_ids, row_home.reshape(1024, 128))
    rows, dense = layer_call(
        layer_input.transpose(0, 2, 1), out_grad.transpose(0, 2, 1), mix_weight, lift_weight.T, linear_weight
    )
    near, far, dense = exchange_call(key, local.reshape(8, 8, 128), rows, dense.reshape(2, 512, 128))
    new_table, new_accum, mix_grad, lift_grad, linear_grad = update_call(
        near, far, dense, table.T, row_accum.reshape(16, 128)
    )
    return (new_table.T, new_accum.reshape(-1), mix_grad, lift_grad.T, linear_grad)


def solution(mesh):
    placed = (
        P(("outer", "inner"), None, None),
        P(("outer", "inner"), None, None),
        P(), P(), P(),
        P(("outer", "inner"), None),
        P(),
        P("inner", None),
        P("inner"),
    )
    return jax.shard_map(
        on_device,
        mesh=mesh,
        in_specs=placed,
        out_specs=(P("inner", None), P("inner"), P(), P(), P()),
        check_vma=False,
    )
```

time: 160 us -> 120 us (0.75); the launches traced: 158 us -> 120 us
  local copies, waits for them, and re-layouts: 26.1 us -> 0 us
  Pallas kernels: 131 us -> 119 us
    unnamed x45 -> x0, local copies, waits for them, and re-layouts: 26.1 us -> none
    pallas_call x2 -> x3, Pallas kernels: 118 us -> 109 us  [the longest x1 88.3 us: exchange_call(): pl.pallas_call(exchange_kernel, out_shape=(jax.ShapeDtypeStruct((2, 2, WI...]
    pallas_call x1, Pallas kernels: 13.2 us -> 10 us  [index_call(): pl.pallas_call(index_kernel, out_shape=(jax.ShapeDtypeStruct((SAMPLES, FE...]
where the time goes in v2:
time: 120 us
  Pallas kernels  119 us (99%)
    pallas_call x1, Pallas kernels, exchange_call(): pl.pallas_call(exchange_kernel, out_shape=(jax.ShapeDtypeStruct((2, 2, WI...  88.3 us
    pallas_call x1, Pallas kernels, layer_call(): pl.pallas_call(layer_kernel, grid=(SAMPLES // TOGETHER,), out_shape=(jax....  16.3 us
    pallas_call x1, Pallas kernels, index_call(): pl.pallas_call(index_kernel, out_shape=(jax.ShapeDtypeStruct((SAMPLES, FE...  10 us
    pallas_call x1, Pallas kernels, update_call(): pl.pallas_call(update_kernel, grid=(4,), out_shape=(jax.ShapeDtypeStruct(...  4.69 us

profile of v2, /device:TPU:15, one launch (start us, length us, event | category | flops | bytes accessed | tf_op | source)
XLA Modules:
  0.0 120.1 jit_solution(7881008666013981907)
XLA Ops:
  0.6 10.0 %index.1 = (s32[32,256]{1,0:T(8,128)}, s32[64,128]{1,0:T(8,128)}) custom-call(s32[32,256]{1,0:T(8,128)} %ids_ref.1, s32[1024,128]{1,0:T(8,128)} %bitcast.19), custom_call_target="tpu_custom_call" | custom-call | tf_op jit(solution)/shard_map/index/pallas_call | solution.py:93
  10.6 16.3 %layer.1 = (bf16[8192,192]{1,0:T(8,128)(2,1)}, f32[1024,128]{1,0:T(8,128)}) custom-call(bf16[32,192,256]{2,1,0:T(8,128)(2,1)} %bitcast.13, bf16[32,192,256]{2,1,0:T(8,128)(2,1)} %bitcast.14, bf16[256,128]{1,0:T(8,128)(2,1)} %mix_ref.1, bf16[192,128]{1,0:T(8,128)(2,1)} %bitcast.20, bf16[256,256]{1,0:T(8,128)(2,1)} %linear_ref.1), custom_call_target="tpu_custom_call" | custom-call | tf_op jit(solution)/shard_map/layer/pallas_call | solution.py:143
  26.9 88.3 %exchange.1 = (bf16[2,2,192,512]{3,2,1,0:T(8,128)(2,1)}, bf16[2,2,192,512]{3,2,1,0:T(8,128)(2,1)}, f32[2,512,128]{2,1,0:T(8,128)}) custom-call(s32[32,256]{1,0:T(8,128)} %get-tuple-element.17.key_ref, s32[8,8,128]{2,1,0:T(8,128)} %bitcast.21, bf16[8192,192]{1,0:T(8,128)(2,1)} %get-tuple-element.19.rows_any, f32[2,512,128]{2,1,0:T(8,128)} %bitcast.18), custom_call_target="tpu_custom_call" | custom-call | tf_op jit(solution)/shard_map/exchange/pallas_call | solution.py:517
  115.2 4.7 %update.1 = (f32[192,2048]{1,0:T(8,128)}, f32[16,128]{1,0:T(8,128)}, f32[256,128]{1,0:T(8,128)}, f32[192,128]{1,0:T(8,128)}, f32[256,256]{1,0:T(8,128)}) custom-call(bf16[4,192,512]{2,1,0:T(8,128)(2,1)} %bitcast.16, bf16[4,192,512]{2,1,0:T(8,128)(2,1)} %bitcast.17, f32[2,512,128]{2,1,0:T(8,128)} %get-tuple-element.23.dense_ref, f32[192,2048]{1,0:T(8,128)} %bitcast.15, ...), custom_call_target="tpu_custom_call" | custom-call | tf_op jit(solution)/shard_map/update/pallas_call | solution.py:577

commit v3 on v2

--- a/solution.py
+++ b/solution.py
@@ -408,7 +408,7 @@
 
     def sort_step(i, carry):
         sort_chunk(i)
-        for k in range(1, 8):
+        for k in (2, 6, 1, 4, 3, 7, 5):
             lookup_copy(i, k).start()
         return carry
 
@@ -428,9 +428,11 @@
         i = 1 + 2 * level + way
         across_copy(i).wait_recv()
         for slot in (1 + 2 * level, 2 + 2 * level):
-            value = pieces(i, (slot + way) % 2)
+            swapped = way == 1 and level < 2
+            value = pieces(i, 1 - slot % 2 if swapped else slot % 2)
             if slot >= 2:
-                value = value + ring_got(way, slot - 2)
+                before = 9 - slot if way == 1 and level == 2 else slot - 2
+                value = value + ring_got(way, before)
             ring_send(way, slot, value)
 
     def sorts(first, last):
@@ -442,37 +444,36 @@
     sorts(0, 1)
     dense_2()
     sorts(1, 4)
+    dense_3()
     for k in range(1, 8):
         index_copy(k).wait_recv()
-    adds(0, 1)
-    dense_3()
-    adds(1, 2)
+    adds(0, 2)
     across_copy(0).wait_recv()
     ring_send(0, 0, pieces(0, 0))
     ring_send(1, 0, pieces(0, 1))
     sorts(4, 5)
     ring_level(0, 0)
     adds(2, 3)
+    dense_4()
     sorts(5, 6)
     ring_level(1, 0)
-    dense_4()
     adds(3, 4)
     sorts(6, 7)
     ring_level(0, 1)
     adds(4, 5)
+    dense_5()
     sorts(7, 8)
     ring_level(1, 1)
-    dense_5()
     adds(5, 6)
     ring_level(0, 2)
+    dense_6()
     adds(6, 7)
     ring_level(1, 2)
-    dense_6()
     adds(7, 8)
     dense_7()
     across_copy(7).wait_recv()
     for p in (1, 0):
-        total = pieces(7, p) + ring_got(0, 6 - p) + ring_got(1, 5 + p)
+        total = pieces(7, p) + ring_got(0, 6 - p) + ring_got(1, 6 - p)
         near[core, p] = total.astype(BF)
         chip_copy(p).start()
         core_copy(p).start()
@@ -553,12 +554,13 @@
 
 def update_kernel(near_ref, far_ref, dense_ref, table_ref, accum_ref, new_table_ref, new_accum_ref, mix_ref, lift_ref, linear_ref):
     step = pl.program_id(0)
-    for q in range(4):
+    for q in range(8):
         block = slice(q * 128, (q + 1) * 128)
-        total = near_ref[0, :, block].astype(F32) + far_ref[0, :, block].astype(F32)
+        part = slice(q % 4 * 128, (q % 4 + 1) * 128)
+        total = near_ref[q // 4, :, part].astype(F32) + far_ref[q // 4, :, part].astype(F32)
         mean = jnp.sum(total * total, axis=0, keepdims=True) * (1.0 / WIDTH)
-        after = accum_ref[pl.ds(step * 4 + q, 1), :] + mean
-        new_accum_ref[pl.ds(step * 4 + q, 1), :] = after
+        after = accum_ref[pl.ds(step * 8 + q, 1), :] + mean
+        new_accum_ref[pl.ds(step * 8 + q, 1), :] = after
         rate = LEARN_RATE / jnp.sqrt(after)
         new_table_ref[:, block] = table_ref[:, block] - total * rate
 
@@ -573,10 +575,10 @@
 
 def update_call(near, far, dense, table, accum):
     whole = lambda *shape: pl.BlockSpec(shape, lambda i: (0,) * len(shape))
-    columns = pl.BlockSpec((WIDTH, PIECE), lambda i: (0, i))
+    columns = pl.BlockSpec((WIDTH, 2 * PIECE), lambda i: (0, i))
     return pl.pallas_call(
         update_kernel,
-        grid=(4,),
+        grid=(2,),
         out_shape=(
             jax.ShapeDtypeStruct((WIDTH, 2048), F32),
             jax.ShapeDtypeStruct((16, 128), F32),
@@ -585,8 +587,8 @@
             jax.ShapeDtypeStruct((256, 256), F32),
         ),
         in_specs=[
-            pl.BlockSpec((1, WIDTH, PIECE), lambda i: (i, 0, 0)),
-            pl.BlockSpec((1, WIDTH, PIECE), lambda i: (i, 0, 0)),
+            pl.BlockSpec((2, WIDTH, PIECE), lambda i: (i, 0, 0)),
+            pl.BlockSpec((2, WIDTH, PIECE), lambda i: (i, 0, 0)),
             whole(2, 512, 128),
             columns,
             whole(16, 128),

time: 120 us -> 114 us (0.950)
  Pallas kernels: 119 us -> 113 us
    pallas_call x1, Pallas kernels: 88.3 us -> 82.9 us  [exchange_call(): pl.pallas_call(exchange_kernel, out_shape=(jax.ShapeDtypeStruct((2, 2, WI...]
    pallas_call x1, Pallas kernels: 4.69 us -> 3.42 us  [update_call(): pl.pallas_call(update_kernel, grid=(2,), out_shape=(jax.ShapeDtypeStruct(...]
where the time goes in v3:
time: 114 us; the launch traced here: 113 us
  Pallas kernels  113 us (99%)
    pallas_call x1, Pallas kernels, exchange_call(): pl.pallas_call(exchange_kernel, out_shape=(jax.ShapeDtypeStruct((2, 2, WI...  82.9 us
    pallas_call x1, Pallas kernels, layer_call(): pl.pallas_call(layer_kernel, grid=(SAMPLES // TOGETHER,), out_shape=(jax....  16.3 us
    pallas_call x1, Pallas kernels, index_call(): pl.pallas_call(index_kernel, out_shape=(jax.ShapeDtypeStruct((SAMPLES, FE...  10 us
    pallas_call x1, Pallas kernels, update_call(): pl.pallas_call(update_kernel, grid=(2,), out_shape=(jax.ShapeDtypeStruct(...  3.42 us

profile of v3, /device:TPU:15, one launch (start us, length us, event | category | flops | bytes accessed | tf_op | source)
XLA Modules:
  0.0 113.4 jit_solution(15410396243463018662)
XLA Ops:
  0.6 10.0 %index.1 = (s32[32,256]{1,0:T(8,128)}, s32[64,128]{1,0:T(8,128)}) custom-call(s32[32,256]{1,0:T(8,128)} %ids_ref.1, s32[1024,128]{1,0:T(8,128)} %bitcast.19), custom_call_target="tpu_custom_call" | custom-call | tf_op jit(solution)/shard_map/index/pallas_call | solution.py:93
  10.6 16.3 %layer.1 = (bf16[8192,192]{1,0:T(8,128)(2,1)}, f32[1024,128]{1,0:T(8,128)}) custom-call(bf16[32,192,256]{2,1,0:T(8,128)(2,1)} %bitcast.13, bf16[32,192,256]{2,1,0:T(8,128)(2,1)} %bitcast.14, bf16[256,128]{1,0:T(8,128)(2,1)} %mix_ref.1, bf16[192,128]{1,0:T(8,128)(2,1)} %bitcast.20, bf16[256,256]{1,0:T(8,128)(2,1)} %linear_ref.1), custom_call_target="tpu_custom_call" | custom-call | tf_op jit(solution)/shard_map/layer/pallas_call | solution.py:143
  26.9 82.9 %exchange.1 = (bf16[2,2,192,512]{3,2,1,0:T(8,128)(2,1)}, bf16[2,2,192,512]{3,2,1,0:T(8,128)(2,1)}, f32[2,512,128]{2,1,0:T(8,128)}) custom-call(s32[32,256]{1,0:T(8,128)} %get-tuple-element.17.key_ref, s32[8,8,128]{2,1,0:T(8,128)} %bitcast.21, bf16[8192,192]{1,0:T(8,128)(2,1)} %get-tuple-element.19.rows_any, f32[2,512,128]{2,1,0:T(8,128)} %bitcast.18), custom_call_target="tpu_custom_call" | custom-call | tf_op jit(solution)/shard_map/exchange/pallas_call | solution.py:518
  109.9 3.4 %update.1 = (f32[192,2048]{1,0:T(8,128)}, f32[16,128]{1,0:T(8,128)}, f32[256,128]{1,0:T(8,128)}, f32[192,128]{1,0:T(8,128)}, f32[256,256]{1,0:T(8,128)}) custom-call(bf16[4,192,512]{2,1,0:T(8,128)(2,1)} %bitcast.16, bf16[4,192,512]{2,1,0:T(8,128)(2,1)} %bitcast.17, f32[2,512,128]{2,1,0:T(8,128)} %get-tuple-element.23.dense_ref, f32[192,2048]{1,0:T(8,128)} %bitcast.15, ...), custom_call_target="tpu_custom_call" | custom-call | tf_op jit(solution)/shard_map/update/pallas_call | solution.py:579
